TPU v7x, 256 devices: a whole 4x4x8 slice. The times are simulated.
256 devices in a mesh: occ: 64 (over x, z, core), aux: 4 (over y).
Axes of the slice: x: 4, y: 4, z: 8, core: 2. Of those that a mesh axis runs over, the one named last changes fastest.
Arguments:
- factors: bfloat16 [128, 256, 1024], P('occ', None, 'aux'), may hold values from -0.8984375 to 0.8984375
- occ_energy: float32 [128], replicated, may hold values from -3 to -0.5
- vir_energy: float32 [256], replicated, may hold values from 0.5 to 3
- i_slot: int32 [2048], P('occ'), may hold values from 0 to 1
- j_slot: int32 [2048], P('occ'), may hold values from 0 to 1
- partner_device: int32 [2048, 1], P('occ'), may hold values from 0 to 63; in each aligned block of 32 rows (0 to 31, 32 to 63, ...) at most 2 rows name the same one
- pair_count: int32 [64], P('occ'), may hold values from 1 to 32, 1843 in all
Outputs:
- gamma: float32 [128, 256, 1024], P('occ', None, 'aux')
- aux_matrix: float32 [1024, 1024], P('aux', 'occ')
Inputs may be any that keep to these rules, and one draw needn't show every extreme that they name: `partner_device`: among the 32 pair slots of one occ index, at most 2 name the same partner device, and some index reaches 2.
All inputs are finite; a program needn't handle non-finite values. No bound on the sum of `pair_count` on one device may be relied on, other than what follows from the above.
Results may differ from a plain program's by a relative error of at most 0.0013.
Values may be sent and summed in bfloat16 or wider, within the bound.
No kernel may reach another device: no remote copies, remote signals or barrier semaphores. Data moves between devices by JAX's collectives and lax.ppermute only.
A program may use at most 128 MiB of HBM per device.

v0:
```python
import jax
import jax.numpy as jnp
from jax import lax
from jax.sharding import PartitionSpec as P


def body(factors, occ_energy, vir_energy, i_slot, j_slot, partner_device, pair_count):
    held, virtuals, columns = factors.shape
    pair_slots = i_slot.shape[0]
    occ_count = lax.axis_size("occ")
    capacity = max(2, (3 * pair_slots // 2 + occ_count - 1) // occ_count)
    slot_total = occ_count * capacity
    device_index = lax.axis_index("occ")
    pair_order = jnp.arange(pair_slots, dtype=jnp.int32)
    living = pair_order < pair_count[0]
    target = partner_device[:, 0]
    earlier = (
        (target[:, None] == target[None, :])
        & living[None, :]
        & (pair_order[None, :] < pair_order[:, None])
    )
    slot_rank = jnp.sum(earlier.astype(jnp.int32), axis=1)
    slot_index = target * capacity + slot_rank
    slot_hit = (slot_index[:, None] == jnp.arange(slot_total, dtype=jnp.int32)[None, :]) & living[
        :, None
    ]
    requests = jnp.sum(jnp.where(slot_hit, j_slot[:, None] + 1, 0), axis=0) - 1
    wanted = lax.all_to_all(requests, "occ", split_axis=0, concat_axis=0, tiled=True)
    wanted_hit = (wanted[:, None] == jnp.arange(held, dtype=jnp.int32)[None, :]).astype(
        jnp.bfloat16
    )
    factor_rows = factors.reshape(held, virtuals * columns)
    far_index = target * held + j_slot
    outgoing = jnp.dot(wanted_hit, factor_rows, preferred_element_type=jnp.float32)
    outgoing = outgoing.astype(jnp.bfloat16).reshape(slot_total, virtuals, columns)
    arrived = lax.all_to_all(outgoing, "occ", split_axis=0, concat_axis=0, tiled=True)
    pick_rows = slot_hit.astype(jnp.bfloat16)
    partner_blocks = jnp.dot(
        pick_rows,
        arrived.reshape(slot_total, virtuals * columns),
        preferred_element_type=jnp.float32,
    )
    partner_blocks = partner_blocks.astype(jnp.bfloat16).reshape(pair_slots, virtuals, columns)
    own_blocks = factors[i_slot]
    orbitals = occ_energy.shape[0]
    table = jnp.arange(orbitals, dtype=jnp.int32)
    own_index = device_index * held + i_slot
    energy_own = jnp.sum(
        jnp.where(own_index[:, None] == table[None, :], occ_energy[None, :], 0.0), axis=1
    )
    energy_far = jnp.sum(
        jnp.where(far_index[:, None] == table[None, :], occ_energy[None, :], 0.0), axis=1
    )
    denominator = (
        vir_energy[None, :, None]
        + vir_energy[None, None, :]
        - energy_own[:, None, None]
        - energy_far[:, None, None]
    )
    partial_value = jnp.einsum(
        "pvq,pwq->pvw", own_blocks, partner_blocks, preferred_element_type=jnp.float32
    )
    summed = lax.psum(partial_value, "aux")
    amplitude = jnp.where(living[:, None, None], summed / denominator, 0.0).astype(jnp.bfloat16)
    local_terms = jnp.einsum(
        "pvw,pwq->pvq", amplitude, partner_blocks, preferred_element_type=jnp.float32
    )
    owner_hit = (i_slot[:, None] == jnp.arange(held, dtype=jnp.int32)[None, :]).astype(jnp.float32)
    gamma_local = jnp.einsum("po,pvq->ovq", owner_hit, local_terms, precision=lax.Precision.HIGHEST)
    return_terms = jnp.einsum(
        "pwv,pwq->pvq", amplitude, own_blocks, preferred_element_type=jnp.float32
    ).astype(jnp.bfloat16)
    placed = jnp.dot(
        slot_hit.astype(jnp.bfloat16).T,
        return_terms.reshape(pair_slots, virtuals * columns),
        preferred_element_type=jnp.float32,
    )
    placed = placed.astype(jnp.bfloat16).reshape(slot_total, virtuals, columns)
    returned = lax.all_to_all(placed, "occ", split_axis=0, concat_axis=0, tiled=True)
    gathered_back = jnp.dot(
        wanted_hit.T,
        returned.reshape(slot_total, virtuals * columns),
        preferred_element_type=jnp.float32,
    )
    gamma = gamma_local + gathered_back.reshape(held, virtuals, columns)
    rounded = gamma.astype(jnp.bfloat16)
    stacked = jnp.stack([rounded, factors])
    gamma_rows = rounded.reshape(held * virtuals, columns)
    factor_flat = factors.reshape(held * virtuals, columns)
    piece = lax.all_gather(stacked, "aux", axis=3, tiled=True)
    width_here = piece.shape[3]
    gamma_piece = piece[0].reshape(held * virtuals, width_here)
    factor_piece = piece[1].reshape(held * virtuals, width_here)
    first = jnp.dot(gamma_rows.T, factor_piece, preferred_element_type=jnp.float32)
    second = jnp.dot(factor_flat.T, gamma_piece, preferred_element_type=jnp.float32)
    terms = first + second
    shared = lax.psum_scatter(terms, "occ", scatter_dimension=1, tiled=True)
    factor_scale = float(orbitals * virtuals) ** (-0.5)
    return (gamma, shared * factor_scale)


def solution(mesh):
    placed = (P("occ", None, "aux"), P(), P(), P("occ"), P("occ"), P("occ", None), P("occ"))
    return jax.shard_map(
        body,
        mesh=mesh,
        in_specs=placed,
        out_specs=(P("occ", None, "aux"), P("aux", "occ")),
        check_vma=False,
    )
```

profile of v0, /device:TPU:8, one launch (start us, length us, event | category | flops | bytes accessed | tf_op | source)
XLA Modules:
  0.0 1268.4 jit_solution(14306813267259421610)
XLA Ops:
  11.0 11.9 all-to-all-start
  24.1 8.2 all-to-all-done
  33.7 8.1 convolution_convert_fusion.1
  41.8 15.6 %copy.41 = bf16[16,8,256,256]{3,2,1,0:T(8,128)(2,1)} copy(bf16[16,8,256,256]{3,1,2,0:T(8,128)(2,1)} %bitcast.69) | data formatting | bytes 33554432
  57.5 6.0 all-to-all-start.1
  66.7 361.4 %all-to-all-done.1 = bf16[128,256,256]{2,1,0:T(8,128)(2,1)} async-done(((bf16[128,256,256]{2,1,0:T(8,128)(2,1)}), bf16[128,256,256]{2,1,0:T(8,128)(2,1)}, u32[]{:S(2)}, u32[]{:S(2)}) %all-to-all-start.1) | async-done | bytes 16777248 | tf_op jit(solution)/shard_map/all_to_all | solution.py:36
  428.1 15.8 %copy.42 = bf16[16,8,256,256]{3,1,2,0:T(8,128)(2,1)S(1)} copy(bf16[16,8,256,256]{3,2,1,0:T(8,128)(2,1)} %bitcast.23) | data formatting | bytes 33554432
  443.9 3.9 convolution_convert_fusion.2
  447.8 3.3 copy.43
  453.1 4.5 fusion.26
  458.6 161.0 %all-reduce.2.cloned.1.call-done = f32[32,256,256]{2,1,0:T(8,128)} async-done(((f32[32,256,256]{2,1,0:T(8,128)}), f32[32,256,256]{2,1,0:T(8,128)}) %all-reduce.2.cloned.1.call-update) | async-done | bytes 8388624 | tf_op jit(solution)/shard_map/psum | solution.py:63
  619.6 5.0 select_convert_fusion
  625.9 4.4 copy.44
  630.3 12.5 convolution_convert_fusion
  642.9 15.6 %copy.45 = bf16[16,8,256,256]{3,2,1,0:T(8,128)(2,1)} copy(bf16[16,8,256,256]{3,1,2,0:T(8,128)(2,1)} %bitcast.68) | data formatting | bytes 33554432
  658.5 10.7 all-to-all-start.2
  669.5 7.9 fusion.27
  677.4 356.4 %all-to-all-done.2 = bf16[128,256,256]{2,1,0:T(8,128)(2,1)} async-done(((bf16[128,256,256]{2,1,0:T(8,128)(2,1)}), bf16[128,256,256]{2,1,0:T(8,128)(2,1)}, u32[]{:S(2)}, u32[]{:S(2)}) %all-to-all-start.2) | async-done | bytes 16777248 | tf_op jit(solution)/shard_map/all_to_all | solution.py:79
  1033.8 23.4 %copy.39 = bf16[128,256,256]{0,2,1:T(8,128)(2,1)} copy(bf16[128,256,256]{2,1,0:T(8,128)(2,1)} %all-to-all-done.2) | data formatting | bytes 33554432 | tf_op jit(solution)/shard_map/reshape | solution.py:82
  1057.3 10.2 fusion
  1067.5 10.6 fusion.25
  1079.7 33.1 %all-gather.2.cloned.1.call-done = bf16[2,2,256,1024]{3,1,2,0:T(2,128)(2,1)} async-done(((bf16[2,2,256,256]{3,1,2,0:T(2,128)(2,1)}), bf16[2,2,256,1024]{3,1,2,0:T(2,128)(2,1)}) %all-gather.2.cloned.1.call-update) | async-done | bytes 2097168 | tf_op jit(solution)/shard_map/all_gather | solution.py:90
  1112.8 2.9 fusion.24
  1119.1 141.2 %reduce-scatter.2.cloned.1.call-done = f32[256,16]{0,1:T(8,128)} async-done(((f32[256,1024]{0,1:T(8,128)}), f32[256,16]{0,1:T(8,128)}) %reduce-scatter.2.cloned.1.call-update) | async-done | bytes 16400 | tf_op jit(solution)/shard_map/reduce_scatter | solution.py:97
  (47 shorter events, 19.8 us)
Async XLA Ops:
  11.0 21.4 %all-to-all-start = ((s32[64,2,1]{1,2,0:T(1,128)}), s32[64,2,1]{1,2,0:T(1,128)S(1)}, u32[]{:S(2)}, u32[]{:S(2)}) async-start(s32[64,2,1]{1,2,0:T(1,128)} %bitcast.5), calls=%async_computation | async-start | bytes 65536 | tf_op jit(solution)/shard_map/all_to_all | solution.py:28
  57.5 6.4 copy-start
  57.5 370.7 %all-to-all-start.1 = ((bf16[128,256,256]{2,1,0:T(8,128)(2,1)}), bf16[128,256,256]{2,1,0:T(8,128)(2,1)}, u32[]{:S(2)}, u32[]{:S(2)}) async-start(bf16[128,256,256]{2,1,0:T(8,128)(2,1)} %bitcast.66), calls=%async_computation.1 | async-start | bytes 33554432 | tf_op jit(solution)/shard_map/all_to_all | solution.py:36
  63.5 556.1 %all-reduce.2.cloned.1.call-start = ((), (), s32[]{:S(2)}) async-start(), calls=%async_computation.4 | async-start | bytes 16777216 | tf_op jit(solution)/shard_map/psum | solution.py:63
  447.8 5.3 copy-start.3
  451.2 1.9 copy-start.2
  457.6 0.7 copy-start.7
  457.6 0.8 copy-start.5
  619.6 5.0 copy-start.4
  624.6 5.7 copy-start.1
  658.5 375.4 %all-to-all-start.2 = ((bf16[128,256,256]{2,1,0:T(8,128)(2,1)}), bf16[128,256,256]{2,1,0:T(8,128)(2,1)}, u32[]{:S(2)}, u32[]{:S(2)}) async-start(bf16[128,256,256]{2,1,0:T(8,128)(2,1)} %bitcast.67), calls=%async_computation.2 | async-start | bytes 33554432 | tf_op jit(solution)/shard_map/all_to_all | solution.py:79
  669.2 443.6 %all-gather.2.cloned.1.call-start = ((), (), s32[]{:S(2)}) async-start(), calls=%async_computation.5 | async-start | bytes 2621440 | tf_op jit(solution)/shard_map/all_gather | solution.py:90
  1057.3 10.2 copy-start.6
  1079.6 180.7 %reduce-scatter.2.cloned.1.call-start = ((), (), s32[]{:S(2)}) async-start(), calls=%async_computation.6 | async-start | bytes 1064960 | tf_op jit(solution)/shard_map/reduce_scatter | solution.py:97
Sparse Core Ops, SparseCore 0:
  457.8 161.7 all-reduce.1
  1079.7 33.0 all-gather.1
  1118.4 141.9 reduce-scatter.1
where the time goes:
time: 1270 us
  waiting for transfers between devices  1060 us (83%)
  local copies, waits for them, and re-layouts  90.8 us (7%)
  matrix products  61 us (5%)
  starting transfers between devices  29.1 us (2%)
  between operations  14.8 us (1%)
    all_to_all x1, waiting for transfers between devices, body(): lax.all_to_all(outgoing, 'occ', split_axis=0, concat_axis=0, tiled=True)  361 us
    all_to_all x1, waiting for transfers between devices, body(): lax.all_to_all(placed, 'occ', split_axis=0, concat_axis=0, tiled=True)  356 us
    psum x1, waiting for transfers between devices, body(): summed = lax.psum(partial_value, 'aux')  161 us
    reduce_scatter x1, waiting for transfers between devices, body(): shared = lax.psum_scatter(terms, 'occ', scatter_dimension=1, tiled=True)  141 us
    unnamed x24, local copies, waits for them, and re-layouts  59.7 us
    all_gather x1, waiting for transfers between devices, body(): piece = lax.all_gather(stacked, 'aux', axis=3, tiled=True)  33.1 us
  transfers between devices with their start and end apart: 6, of which 6 were waited for; matrix products, arithmetic and copies ran while one was open for 1% of the time, Pallas kernels for 0%

commit v1 on v0

--- a/solution.py
+++ b/solution.py
@@ -2,6 +2,7 @@
 import jax.numpy as jnp
 from jax import lax
 from jax.sharding import PartitionSpec as P
+from jax.lax import all_gather
 
 
 def body(factors, occ_energy, vir_energy, i_slot, j_slot, partner_device, pair_count):
@@ -60,7 +61,7 @@
     partial_value = jnp.einsum(
         "pvq,pwq->pvw", own_blocks, partner_blocks, preferred_element_type=jnp.float32
     )
-    summed = lax.psum(partial_value, "aux")
+    summed = jnp.sum(all_gather(partial_value, "aux"), axis=0)
     amplitude = jnp.where(living[:, None, None], summed / denominator, 0.0).astype(jnp.bfloat16)
     local_terms = jnp.einsum(
         "pvw,pwq->pvq", amplitude, partner_blocks, preferred_element_type=jnp.float32

time: 1270 us -> 1420 us (1.12)
  waiting for transfers between devices: 1060 us -> 1190 us
  other arithmetic: 11.3 us -> 26.9 us
    all_gather x0 -> x1, waiting for transfers between devices: none -> 293 us  [body(): summed = jnp.sum(all_gather(partial_value, 'aux'), axis=0)]
    psum x1 -> x0, waiting for transfers between devices: 161 us -> none  [body(): summed = lax.psum(partial_value, 'aux')]
    reduce_sum x0 -> x1, other arithmetic: none -> 16 us  [body(): summed = jnp.sum(all_gather(partial_value, 'aux'), axis=0)]
where the time goes in v1:
time: 1420 us
  waiting for transfers between devices  1190 us (84%)
  local copies, waits for them, and re-layouts  90.8 us (6%)
  matrix products  61 us (4%)
  starting transfers between devices  29.3 us (2%)
  other arithmetic  26.9 us (2%)
  between operations  14.9 us (1%)
    all_to_all x1, waiting for transfers between devices, body(): lax.all_to_all(outgoing, 'occ', split_axis=0, concat_axis=0, tiled=True)  361 us
    all_to_all x1, waiting for transfers between devices, body(): lax.all_to_all(placed, 'occ', split_axis=0, concat_axis=0, tiled=True)  356 us
    all_gather x1, waiting for transfers between devices, body(): summed = jnp.sum(all_gather(partial_value, 'aux'), axis=0)  293 us
    reduce_scatter x1, waiting for transfers between devices, body(): shared = lax.psum_scatter(terms, 'occ', scatter_dimension=1, tiled=True)  141 us
    unnamed x24, local copies, waits for them, and re-layouts  59.7 us
    all_gather x1, waiting for transfers between devices, body(): piece = lax.all_gather(stacked, 'aux', axis=3, tiled=True)  33.1 us
  transfers between devices with their start and end apart: 6, of which 6 were waited for; matrix products, arithmetic and copies ran while one was open for 1% of the time, Pallas kernels for 0%

profile of v1, /device:TPU:8, one launch (start us, length us, event | category | flops | bytes accessed | tf_op | source)
XLA Modules:
  0.0 1416.3 jit_solution(14598139161936386033)
XLA Ops:
  11.0 11.9 all-to-all-start
  24.1 8.2 all-to-all-done
  33.7 8.1 convolution_convert_fusion.1
  41.8 15.6 %copy.39 = bf16[16,8,256,256]{3,2,1,0:T(8,128)(2,1)} copy(bf16[16,8,256,256]{3,1,2,0:T(8,128)(2,1)} %bitcast.70) | data formatting | bytes 33554432
  57.5 6.0 all-to-all-start.1
  66.8 361.3 %all-to-all-done.1 = bf16[128,256,256]{2,1,0:T(8,128)(2,1)} async-done(((bf16[128,256,256]{2,1,0:T(8,128)(2,1)}), bf16[128,256,256]{2,1,0:T(8,128)(2,1)}, u32[]{:S(2)}, u32[]{:S(2)}) %all-to-all-start.1) | async-done | bytes 16777248 | tf_op jit(solution)/shard_map/all_to_all | solution.py:37
  428.1 15.8 %copy.40 = bf16[16,8,256,256]{3,1,2,0:T(8,128)(2,1)S(1)} copy(bf16[16,8,256,256]{3,2,1,0:T(8,128)(2,1)} %bitcast.24) | data formatting | bytes 33554432
  443.9 3.9 convolution_convert_fusion.2
  447.8 3.3 copy.41
  453.1 4.5 fusion.26
  458.6 293.2 %all-gather.6.cloned.1.call-done = f32[128,256,256]{2,1,0:T(8,128)} async-done(((f32[32,256,256]{2,1,0:T(8,128)}), f32[128,256,256]{2,1,0:T(8,128)}) %all-gather.6.cloned.1.call-update) | async-done | bytes 33554448 | tf_op jit(solution)/shard_map/all_gather | solution.py:64
  751.8 16.0 %reduce_sum.50 = f32[32,256,256]{2,1,0:T(8,128)} reduce(f32[4,32,256,256]{3,2,1,0:T(8,128)} %bitcast.74, f32[]{:T(128)} %constant.5.clone.1), dimensions={0}, to_apply=%region_2.3 | reduce | flops 6291456 | bytes 41943044 | tf_op jit(solution)/shard_map/reduce_sum | solution.py:64
  767.8 4.7 select_convert_fusion
  773.8 4.4 copy.42
  778.2 12.5 convolution_convert_fusion
  790.7 15.6 %copy.43 = bf16[16,8,256,256]{3,2,1,0:T(8,128)(2,1)} copy(bf16[16,8,256,256]{3,1,2,0:T(8,128)(2,1)} %bitcast.69) | data formatting | bytes 33554432
  806.3 10.7 all-to-all-start.2
  817.3 7.9 fusion.27
  825.3 356.4 %all-to-all-done.2 = bf16[128,256,256]{2,1,0:T(8,128)(2,1)} async-done(((bf16[128,256,256]{2,1,0:T(8,128)(2,1)}), bf16[128,256,256]{2,1,0:T(8,128)(2,1)}, u32[]{:S(2)}, u32[]{:S(2)}) %all-to-all-start.2) | async-done | bytes 16777248 | tf_op jit(solution)/shard_map/all_to_all | solution.py:80
  1181.7 23.5 %copy.37 = bf16[128,256,256]{0,2,1:T(8,128)(2,1)} copy(bf16[128,256,256]{2,1,0:T(8,128)(2,1)} %all-to-all-done.2) | data formatting | bytes 33554432 | tf_op jit(solution)/shard_map/reshape | solution.py:83
  1205.2 10.2 fusion
  1215.4 10.6 fusion.25
  1227.6 33.1 %all-gather.4.cloned.1.call-done = bf16[2,2,256,1024]{3,1,2,0:T(2,128)(2,1)} async-done(((bf16[2,2,256,256]{3,1,2,0:T(2,128)(2,1)}), bf16[2,2,256,1024]{3,1,2,0:T(2,128)(2,1)}) %all-gather.4.cloned.1.call-update) | async-done | bytes 2097168 | tf_op jit(solution)/shard_map/all_gather | solution.py:91
  1267.0 141.2 %reduce-scatter.2.cloned.1.call-done = f32[256,16]{0,1:T(8,128)} async-done(((f32[256,1024]{0,1:T(8,128)}), f32[256,16]{0,1:T(8,128)}) %reduce-scatter.2.cloned.1.call-update) | async-done | bytes 16400 | tf_op jit(solution)/shard_map/reduce_scatter | solution.py:98
  (48 shorter events, 22.8 us)
Async XLA Ops:
  11.0 21.4 %all-to-all-start = ((s32[64,2,1]{1,2,0:T(1,128)}), s32[64,2,1]{1,2,0:T(1,128)S(1)}, u32[]{:S(2)}, u32[]{:S(2)}) async-start(s32[64,2,1]{1,2,0:T(1,128)} %bitcast.5), calls=%async_computation | async-start | bytes 65536 | tf_op jit(solution)/shard_map/all_to_all | solution.py:29
  57.5 6.6 copy-start
  57.5 370.7 %all-to-all-start.1 = ((bf16[128,256,256]{2,1,0:T(8,128)(2,1)}), bf16[128,256,256]{2,1,0:T(8,128)(2,1)}, u32[]{:S(2)}, u32[]{:S(2)}) async-start(bf16[128,256,256]{2,1,0:T(8,128)(2,1)} %bitcast.67), calls=%async_computation.1 | async-start | bytes 33554432 | tf_op jit(solution)/shard_map/all_to_all | solution.py:37
  63.5 688.3 %all-gather.6.cloned.1.call-start = ((), (), s32[]{:S(2)}) async-start(), calls=%async_computation.6 | async-start | bytes 41943040 | tf_op jit(solution)/shard_map/all_gather | solution.py:64
  447.8 5.3 copy-start.3
  451.2 1.9 copy-start.2
  457.6 0.7 copy-start.7
  457.6 0.8 copy-start.5
  767.8 4.7 copy-start.4
  772.4 5.7 copy-start.1
  806.3 375.4 %all-to-all-start.2 = ((bf16[128,256,256]{2,1,0:T(8,128)(2,1)}), bf16[128,256,256]{2,1,0:T(8,128)(2,1)}, u32[]{:S(2)}, u32[]{:S(2)}) async-start(bf16[128,256,256]{2,1,0:T(8,128)(2,1)} %bitcast.68), calls=%async_computation.2 | async-start | bytes 33554432 | tf_op jit(solution)/shard_map/all_to_all | solution.py:80
  817.0 443.7 %all-gather.4.cloned.1.call-start = ((), (), s32[]{:S(2)}) async-start(), calls=%async_computation.4 | async-start | bytes 2621440 | tf_op jit(solution)/shard_map/all_gather | solution.py:91
  1205.2 10.2 copy-start.6
  1227.5 180.7 %reduce-scatter.2.cloned.1.call-start = ((), (), s32[]{:S(2)}) async-start(), calls=%async_computation.5 | async-start | bytes 1064960 | tf_op jit(solution)/shard_map/reduce_scatter | solution.py:98
Sparse Core Ops, SparseCore 0:
  457.8 293.9 all-gather.5
  1227.6 33.0 all-gather.3
  1266.3 141.8 reduce-scatter.1
